TPU v7x, 256 devices: a whole 4x4x8 slice. The times are simulated.
256 devices in a mesh: row: 16 (over z, core), col: 16 (over y, x).
Axes of the slice: x: 4, y: 4, z: 8, core: 2. Of those that a mesh axis runs over, the one named last changes fastest.
Arguments:
- start_basis: float32 [32, 131072], P(None, ('row', 'col')), may hold values from -6 to 6
- degrees: float32 [131072], P(('row', 'col')), may hold values from 0.5 to 1.5
- tiles: float32 [8192, 256, 256], P(('row', 'col')), may hold values from -0.046875 to 0.046875
- tile_rows: int32 [16, 512], P('row', 'col'), may hold values from 0 to 31, as said below
- tile_cols: int32 [16, 512], P('row', 'col'), may hold values from 0 to 31
- counts: int32 [16, 16], P('row', 'col'), may hold values from 1 to 31, as said below
Outputs:
- basis: float32 [32, 131072], P(None, ('row', 'col'))
- projected: float32 [32, 32], replicated
Inputs may be any that keep to these rules, and one draw needn't show every extreme that they name: `tile_rows`: the 32 (row, column) pairs of one device are distinct. counts[r, c] + counts[r', c] <= 32 where r' differs from r by 8; equality holds in column 0.
All inputs are finite; a program needn't handle non-finite values.
Results may differ from a plain program's by a relative error of at most 0.0003.
Values sent between devices are 32-bit elements; how exact they have to be, the bound alone decides.
A program may use at most 64 MiB of HBM per device.

v0:
```python
import jax
import jax.numpy as jnp
from jax import lax
from jax.sharding import PartitionSpec as P

DEGREE = 3
center_shift = 1.0
spread_radius = 1.4
group_width = 8


def tile_products(blocks, tiles, row_local, col_local, live, row_blocks):
    subspace = blocks.shape[0]
    edge = blocks.shape[2]
    block_ids = jnp.arange(row_blocks, dtype=jnp.int32)

    def add_group(index, total):
        start = index * group_width
        group_tiles = lax.dynamic_slice_in_dim(tiles, start, group_width, 0)
        group_rows = lax.dynamic_slice_in_dim(row_local, start, group_width, 0)
        group_cols = lax.dynamic_slice_in_dim(col_local, start, group_width, 0)
        picked = jnp.take(blocks, group_cols, axis=1)
        product = jnp.einsum("kgj,gij->kgi", picked, group_tiles, precision=lax.Precision.HIGHEST)
        valid = start + jnp.arange(group_width, dtype=jnp.int32) < live
        select = ((group_rows[None, :] == block_ids[:, None]) & valid[None, :]).astype(jnp.float32)
        return total + jnp.einsum("ig,kgb->kib", select, product, precision=lax.Precision.HIGHEST)

    initial = jnp.zeros((subspace, row_blocks, edge), jnp.float32)
    return lax.fori_loop(0, (live + group_width - 1) // group_width, add_group, initial)


def inner_products(left, right):
    return jnp.einsum("kn,mn->km", left, right, precision=lax.Precision.HIGHEST)


def body(start_basis, degrees, tiles, tile_rows, tile_cols, counts):
    subspace = start_basis.shape[0]
    edge = tiles.shape[1]
    row_local = tile_rows[0]
    col_local = tile_cols[0]
    live_count = counts[0, 0]
    row_blocks = lax.axis_size("col") * start_basis.shape[1] // edge
    nverts = lax.axis_size("row") * lax.axis_size("col") * start_basis.shape[1]

    def apply_operator(vectors):
        gathered = lax.all_gather(vectors, "row", axis=1, tiled=True)
        blocks = gathered.reshape(subspace, -1, edge)
        partial_value = tile_products(blocks, tiles, row_local, col_local, live_count, row_blocks)
        summed = lax.psum_scatter(
            partial_value.reshape(subspace, -1), "col", scatter_dimension=1, tiled=True
        )
        return degrees[None, :] * vectors - summed

    def shifted(vectors):
        return (apply_operator(vectors) - center_shift * vectors) / spread_radius

    previous = start_basis
    filtered = shifted(start_basis)
    for level in range(DEGREE - 1):
        following = 2.0 * shifted(filtered) - previous
        previous, filtered = (filtered, following)
    gram_matrix = lax.psum(inner_products(filtered, filtered), ("row", "col")) / nverts
    factor = jnp.linalg.cholesky(gram_matrix)
    basis = jax.scipy.linalg.solve_triangular(factor, filtered, lower=True)
    image = apply_operator(basis)
    moment = lax.psum(inner_products(basis, image), ("row", "col")) / nverts
    projected = 0.5 * (moment + moment.T)
    return (basis, projected)


def solution(mesh):
    return jax.shard_map(
        body,
        mesh=mesh,
        in_specs=(
            P(None, ("row", "col")),
            P(("row", "col")),
            P(("row", "col"), None, None),
            P("row", "col"),
            P("row", "col"),
            P("row", "col"),
        ),
        out_specs=(P(None, ("row", "col")), P()),
        check_vma=False,
    )
```

profile of v0, /device:TPU:1, one launch (start us, length us, event | category | flops | bytes accessed | tf_op | source)
XLA Modules:
  0.0 776.5 jit_solution(2379847340742066916)
XLA Ops:
  8.6 44.0 %all-gather.5.cloned.1.call-done = f32[32,8192]{1,0:T(8,128)} async-done(((f32[32,512]{1,0:T(8,128)}), f32[32,8192]{1,0:T(8,128)}) %all-gather.5.cloned.1.call-update) | async-done | bytes 1048592 | tf_op jit(solution)/shard_map/all_gather | solution.py:46
  52.6 1.4 copy.59
  54.1 29.0 %while.44 = (s32[]{:T(128)}, f32[32,32,256]{2,1,0:T(8,128)S(1)}, s32[]{:T(128)}, f32[32,256,256]{2,1,0:T(8,128)}, s32[32]{0:T(128)}, /*index=5*/f32[32,32,256]{2...) while((s32[]{:T(128)}, f32[32,32,256]{2,1,0:T(8,128)S(1)}, ...), condition=%wide.region_1.3_spmd.clone, body=%wide.region_0.2_spmd.clone.sunk | while | flops 226821696 | bytes 5509559 | solution.py:29
  54.1 1.4 compare_and_fusion.8
  56.1 3.6 fusion.122
  61.4 1.4 compare_and_fusion.8
  63.4 3.6 fusion.122
  67.7 0.9 fusion.123
  68.6 1.4 compare_and_fusion.8
  70.6 3.6 fusion.122
  75.9 1.4 compare_and_fusion.8
  77.9 3.6 fusion.122
  83.1 1.6 copy.40
  84.8 75.6 %reduce-scatter.5.cloned.1.call-done = f32[32,512]{1,0:T(8,128)} async-done(((f32[32,8192]{1,0:T(8,128)}), f32[32,512]{1,0:T(8,128)}) %reduce-scatter.5.cloned.1.call-update) | async-done | bytes 65552 | tf_op jit(solution)/shard_map/reduce_scatter | solution.py:49
  160.4 1.5 fusion.83
  161.9 41.0 %all-gather.7.cloned.1.call-done = f32[32,8192]{1,0:T(8,128)} async-done(((f32[32,512]{1,0:T(8,128)}), f32[32,8192]{1,0:T(8,128)}) %all-gather.7.cloned.1.call-update) | async-done | bytes 1048592 | tf_op jit(solution)/shard_map/all_gather | solution.py:46
  202.9 1.4 copy.58
  204.4 29.0 %while.45 = (s32[]{:T(128)}, f32[32,32,256]{2,1,0:T(8,128)S(1)}, s32[]{:T(128)}, f32[32,256,256]{2,1,0:T(8,128)}, s32[32]{0:T(128)}, /*index=5*/f32[32,32,256]{2...) while((s32[]{:T(128)}, f32[32,32,256]{2,1,0:T(8,128)S(1)}, ...), condition=%wide.region_4.6_spmd.clone, body=%wide.region_3.5_spmd.clone.sunk | while | flops 226821696 | bytes 5509559 | solution.py:29
  204.4 1.4 compare_and_fusion.9
  206.4 3.6 fusion.128
  210.8 0.9 fusion.129
  211.7 1.4 compare_and_fusion.9
  213.6 3.6 fusion.128
  218.9 1.4 compare_and_fusion.9
  220.9 3.6 fusion.128
  226.2 1.4 compare_and_fusion.9
  228.1 3.6 fusion.128
  233.4 1.6 copy.41
  235.1 75.6 %reduce-scatter.7.cloned.1.call-done = f32[32,512]{1,0:T(8,128)} async-done(((f32[32,8192]{1,0:T(8,128)}), f32[32,512]{1,0:T(8,128)}) %reduce-scatter.7.cloned.1.call-update) | async-done | bytes 65552 | tf_op jit(solution)/shard_map/reduce_scatter | solution.py:49
  310.7 1.5 multiply_subtract_fusion.1
  312.3 40.8 %all-gather.9.cloned.1.call-done = f32[32,8192]{1,0:T(8,128)} async-done(((f32[32,512]{1,0:T(8,128)}), f32[32,8192]{1,0:T(8,128)}) %all-gather.9.cloned.1.call-update) | async-done | bytes 1048592 | tf_op jit(solution)/shard_map/all_gather | solution.py:46
  353.1 1.4 copy.57
  354.6 29.0 %while.46 = (s32[]{:T(128)}, f32[32,32,256]{2,1,0:T(8,128)S(1)}, s32[]{:T(128)}, f32[32,256,256]{2,1,0:T(8,128)}, s32[32]{0:T(128)}, /*index=5*/f32[32,32,256]{2...) while((s32[]{:T(128)}, f32[32,32,256]{2,1,0:T(8,128)S(1)}, ...), condition=%wide.region_7.9_spmd.clone, body=%wide.region_6.8_spmd.clone.sunk | while | flops 226821696 | bytes 5509559 | solution.py:29
  354.6 1.4 compare_and_fusion.10
  356.6 3.6 fusion.134
  361.9 1.4 compare_and_fusion.10
  363.8 3.6 fusion.134
  369.1 1.4 compare_and_fusion.10
  371.1 3.6 fusion.134
  376.4 1.4 compare_and_fusion.10
  378.3 3.6 fusion.134
  382.7 0.9 fusion.135
  383.6 1.6 copy.42
  385.3 75.6 %reduce-scatter.9.cloned.1.call-done = f32[32,512]{1,0:T(8,128)} async-done(((f32[32,8192]{1,0:T(8,128)}), f32[32,512]{1,0:T(8,128)}) %reduce-scatter.9.cloned.1.call-update) | async-done | bytes 65552 | tf_op jit(solution)/shard_map/reduce_scatter | solution.py:49
  462.0 77.5 %psum.14 = f32[32,32]{0,1:T(8,128)S(1)} all-reduce(f32[32,32]{0,1:T(8,128)S(1)} %fusion.89), channel_id=1, replica_groups=mesh['row'=16,'col'=16] {'row','col'}, use_global_device_ids=true, to_apply=%region_9.11 | all-reduce | flops 1024 | bytes 8192 | tf_op jit(solution)/shard_map/psum | solution.py:62
  539.6 2.9 cholesky.16
  543.9 2.4 custom-call.7
  546.3 0.9 fusion.87
  547.3 35.6 %all-gather.11.cloned.1.call-done = f32[32,8192]{1,0:T(8,128)} async-done(((f32[32,512]{1,0:T(8,128)}), f32[32,8192]{1,0:T(8,128)}) %all-gather.11.cloned.1.call-update) | async-done | bytes 1048592 | tf_op jit(solution)/shard_map/all_gather | solution.py:46
  582.9 1.4 copy.56
  584.4 29.0 %while.47 = (s32[]{:T(128)}, f32[32,32,256]{2,1,0:T(8,128)S(1)}, s32[]{:T(128)}, f32[32,256,256]{2,1,0:T(8,128)}, s32[32]{0:T(128)}, /*index=5*/f32[32,32,256]{2...) while((s32[]{:T(128)}, f32[32,32,256]{2,1,0:T(8,128)S(1)}, ...), condition=%wide.region_13.15_spmd.clone, body=%wide.region_12.14_spmd.clone.sunk | while | flops 226821696 | bytes 5509559 | solution.py:29
  584.4 1.4 compare_and_fusion.11
  586.4 3.6 fusion.140
  590.8 0.9 fusion.141
  591.7 1.4 compare_and_fusion.11
  593.6 3.6 fusion.140
  598.9 1.4 compare_and_fusion.11
  600.9 3.6 fusion.140
  606.2 1.4 compare_and_fusion.11
  608.1 3.6 fusion.140
  613.4 1.6 copy.43
  615.0 75.7 %reduce-scatter.11.cloned.1.call-done = f32[32,512]{1,0:T(8,128)} async-done(((f32[32,8192]{1,0:T(8,128)}), f32[32,512]{1,0:T(8,128)}) %reduce-scatter.11.cloned.1.call-update) | async-done | bytes 65552 | tf_op jit(solution)/shard_map/reduce_scatter | solution.py:49
  690.7 1.0 fusion.80
  691.7 77.3 %psum.15 = f32[32,32]{0,1:T(8,128)S(1)} all-reduce(f32[32,32]{0,1:T(8,128)S(1)} %fusion.80), channel_id=1, replica_groups=mesh['row'=16,'col'=16] {'row','col'}, use_global_device_ids=true, to_apply=%region_15.17 | all-reduce | flops 1024 | bytes 8192 | tf_op jit(solution)/shard_map/psum | solution.py:66
  (104 shorter events, 36.3 us)
Async XLA Ops:
  7.2 45.4 %all-gather.5.cloned.1.call-start = ((), (), s32[]{:S(2)}) async-start(), calls=%async_computation.4 | async-start | bytes 1114112 | tf_op jit(solution)/shard_map/all_gather | solution.py:46
  7.9 152.5 %reduce-scatter.5.cloned.1.call-start = ((), (), s32[]{:S(2)}) async-start(), calls=%async_computation.5 | async-start | bytes 1114112 | tf_op jit(solution)/shard_map/reduce_scatter | solution.py:49
  54.1 106.3 %copy-start = (f32[32,512]{1,0:T(8,128)S(1)}, f32[32,512]{1,0:T(8,128)}, u32[]{:S(2)}) copy-start(f32[32,512]{1,0:T(8,128)} %param.16) | copy-start | bytes 196612
  54.1 106.3 %copy-start.4 = (f32[512]{0:T(512)S(1)}, f32[512]{0:T(512)}, u32[]{:S(2)}) copy-start(f32[512]{0:T(512)} %param.17) | copy-start | bytes 6148
  84.7 118.2 %all-gather.7.cloned.1.call-start = ((), (), s32[]{:S(2)}) async-start(), calls=%async_computation.6 | async-start | bytes 1114112 | tf_op jit(solution)/shard_map/all_gather | solution.py:46
  161.9 148.8 %reduce-scatter.7.cloned.1.call-start = ((), (), s32[]{:S(2)}) async-start(), calls=%async_computation.7 | async-start | bytes 1114112 | tf_op jit(solution)/shard_map/reduce_scatter | solution.py:49
  204.4 106.3 %copy-start.2 = (f32[32,512]{1,0:T(8,128)S(1)}, f32[32,512]{1,0:T(8,128)}, u32[]{:S(2)}) copy-start(f32[32,512]{1,0:T(8,128)} %reduce-scatter.5.cloned.1.call-done) | copy-start | bytes 196612
  235.0 118.1 %all-gather.9.cloned.1.call-start = ((), (), s32[]{:S(2)}) async-start(), calls=%async_computation.8 | async-start | bytes 1114112 | tf_op jit(solution)/shard_map/all_gather | solution.py:46
  312.2 148.7 %reduce-scatter.9.cloned.1.call-start = ((), (), s32[]{:S(2)}) async-start(), calls=%async_computation.9 | async-start | bytes 1114112 | tf_op jit(solution)/shard_map/reduce_scatter | solution.py:49
  354.6 106.3 %copy-start.3 = (f32[32,512]{1,0:T(8,128)S(1)}, f32[32,512]{1,0:T(8,128)}, u32[]{:S(2)}) copy-start(f32[32,512]{1,0:T(8,128)} %multiply_subtract_fusion.1) | copy-start | bytes 196612
  385.2 197.7 %all-gather.11.cloned.1.call-start = ((), (), s32[]{:S(2)}) async-start(), calls=%async_computation.10 | async-start | bytes 1114112 | tf_op jit(solution)/shard_map/all_gather | solution.py:46
  547.2 143.5 %reduce-scatter.11.cloned.1.call-start = ((), (), s32[]{:S(2)}) async-start(), calls=%async_computation.11 | async-start | bytes 1114112 | tf_op jit(solution)/shard_map/reduce_scatter | solution.py:49
  584.4 106.3 %copy-start.1 = (f32[32,512]{1,0:T(8,128)S(1)}, f32[32,512]{1,0:T(8,128)}, u32[]{:S(2)}) copy-start(f32[32,512]{1,0:T(8,128)} %fusion.87) | copy-start | bytes 196612
Sparse Core Ops, SparseCore 0:
  9.8 42.7 all-gather.4
  84.9 75.4 reduce-scatter.4
  162.8 40.0 all-gather.6
  235.1 75.5 reduce-scatter.6
  313.0 40.0 all-gather.8
  385.3 75.5 reduce-scatter.8
  547.4 35.5 all-gather.10
  615.1 75.4 reduce-scatter.10
where the time goes:
time: 778 us; the launch traced here: 777 us
  waiting for transfers between devices  465 us (60%)
  blocking collectives  155 us (20%)
  matrix products  74.3 us (10%)
  other arithmetic  33.4 us (4%)
  local copies, waits for them, and re-layouts  33.2 us (4%)
  between operations  15 us (2%)
    reduce_scatter x4, waiting for transfers between devices, apply_operator(): lax.psum_scatter(partial_value.reshape(subspace, -1), 'col', scatter_dime...  303 us
    all_gather x4, waiting for transfers between devices, apply_operator(): gathered = lax.all_gather(vectors, 'row', axis=1, tiled=True)  161 us
    psum x1, blocking collectives, body(): lax.psum(inner_products(filtered, filtered), ('row', 'col')) / nverts  77.5 us
    psum x1, blocking collectives, body(): moment = lax.psum(inner_products(basis, image), ('row', 'col')) / nverts  77.3 us
    dot_general x16, matrix products, add_group(): jnp.einsum('kgj,gij->kgi', picked, group_tiles, precision=lax.Precision.H...  58.1 us
    and x16, other arithmetic, add_group(): picked = jnp.take(blocks, group_cols, axis=1)  22.1 us
  transfers between devices with their start and end apart: 8, of which 8 were waited for; matrix products, arithmetic and copies ran while one was open for 0% of the time, Pallas kernels for 0%

commit v1 on v0

--- a/solution.py
+++ b/solution.py
@@ -43,7 +43,9 @@
     nverts = lax.axis_size("row") * lax.axis_size("col") * start_basis.shape[1]
 
     def apply_operator(vectors):
-        gathered = lax.all_gather(vectors, "row", axis=1, tiled=True)
+        gathered = jnp.concatenate(
+            lax.all_to_all(jnp.stack([vectors] * lax.axis_size("row")), "row", 0, 0), axis=1
+        )
         blocks = gathered.reshape(subspace, -1, edge)
         partial_value = tile_products(blocks, tiles, row_local, col_local, live_count, row_blocks)
         summed = lax.psum_scatter(

time: 778 us -> 733 us (0.942)
  waiting for transfers between devices: 465 us -> 402 us
  starting transfers between devices: 0.32 us -> 35.6 us
  other arithmetic: 33.4 us -> 21.7 us
    all_gather x4 -> x0, waiting for transfers between devices: 161 us -> none  [apply_operator(): gathered = lax.all_gather(vectors, 'row', axis=1, tiled=True)]
    all_to_all x0 -> x4, waiting for transfers between devices: none -> 111 us  [apply_operator(): lax.all_to_all(jnp.stack([vectors] * lax.axis_size('row')), 'row', 0, 0)]
    all_to_all x0 -> x4, starting transfers between devices: none -> 35.3 us  [apply_operator(): lax.all_to_all(jnp.stack([vectors] * lax.axis_size('row')), 'row', 0, 0)]
    reduce_scatter x4, waiting for transfers between devices: 303 us -> 291 us  [apply_operator(): lax.psum_scatter(partial_value.reshape(subspace, -1), 'col', scatter_dime...]
    and x16, other arithmetic: 22.1 us -> 11.6 us  [add_group(): picked = jnp.take(blocks, group_cols, axis=1)]
    dynamic_slice x16, local copies, waits for them, and re-layouts: 11.7 us -> 1.26 us  [add_group(): group_rows = lax.dynamic_slice_in_dim(row_local, start, group_width, 0)]
where the time goes in v1:
time: 733 us; the launch traced here: 731 us
  waiting for transfers between devices  402 us (55%)
  blocking collectives  155 us (21%)
  matrix products  73.7 us (10%)
  starting transfers between devices  35.6 us (5%)
  local copies, waits for them, and re-layouts  28.1 us (4%)
  other arithmetic  21.7 us (3%)
  between operations  14.7 us (2%)
    reduce_scatter x4, waiting for transfers between devices, apply_operator(): lax.psum_scatter(partial_value.reshape(subspace, -1), 'col', scatter_dime...  291 us
    all_to_all x4, waiting for transfers between devices, apply_operator(): lax.all_to_all(jnp.stack([vectors] * lax.axis_size('row')), 'row', 0, 0)  111 us
    psum x1, blocking collectives, body(): moment = lax.psum(inner_products(basis, image), ('row', 'col')) / nverts  77.3 us
    psum x1, blocking collectives, body(): lax.psum(inner_products(filtered, filtered), ('row', 'col')) / nverts  77.3 us
    dot_general x16, matrix products, add_group(): jnp.einsum('kgj,gij->kgi', picked, group_tiles, precision=lax.Precision.H...  58.1 us
    all_to_all x4, starting transfers between devices, apply_operator(): lax.all_to_all(jnp.stack([vectors] * lax.axis_size('row')), 'row', 0, 0)  35.3 us
  transfers between devices with their start and end apart: 8, of which 8 were waited for; matrix products, arithmetic and copies ran while one was open for 0% of the time, Pallas kernels for 0%

profile of v1, /device:TPU:1, one launch (start us, length us, event | category | flops | bytes accessed | tf_op | source)
XLA Modules:
  0.0 731.2 jit_solution(10093240371446845267)
XLA Ops:
  7.2 2.0 stack.8
  9.1 10.0 %all-to-all-start = ((f32[16,32,512]{2,1,0:T(8,128)}), f32[16,32,512]{2,1,0:T(8,128)S(1)}, u32[]{:S(2)}, u32[]{:S(2)}) async-start(f32[16,32,512]{2,1,0:T(8,128)} %stack.8), calls=%async_computation | async-start | bytes 2097152 | tf_op jit(solution)/shard_map/all_to_all | solution.py:47
  19.8 27.3 %all-to-all-done = f32[16,32,512]{2,1,0:T(8,128)S(1)} async-done(((f32[16,32,512]{2,1,0:T(8,128)}), f32[16,32,512]{2,1,0:T(8,128)S(1)}, u32[]{:S(2)}, u32[]{:S(2)}) %all-to-all-start) | async-done | bytes 1048608 | tf_op jit(solution)/shard_map/all_to_all | solution.py:47
  48.7 23.8 %while.44 = (s32[]{:T(128)}, f32[32,32,256]{2,1,0:T(8,128)S(1)}, s32[]{:T(128)}, f32[32,256,256]{2,1,0:T(8,128)}, s32[32]{0:T(128)S(1)}, /*index=5*/f32[32,32,25...) while((s32[]{:T(128)}, f32[32,32,256]{2,1,0:T(8,128)S(1)}, ...), condition=%wide.region_1.3_spmd.clone, body=%wide.region_0.2_spmd.clone.sunk | while | flops 226821696 | bytes 5509559 | solution.py:29
  50.0 3.6 fusion.122
  53.7 0.9 fusion.123
  55.9 3.6 fusion.122
  59.7 0.9 fusion.123
  61.9 3.6 fusion.122
  65.6 0.9 fusion.123
  67.8 3.6 fusion.122
  71.5 0.9 fusion.123
  72.4 1.6 copy.50
  74.1 74.8 %reduce-scatter.5.cloned.1.call-done = f32[32,512]{1,0:T(8,128)} async-done(((f32[32,8192]{1,0:T(8,128)}), f32[32,512]{1,0:T(8,128)}) %reduce-scatter.5.cloned.1.call-update) | async-done | bytes 65552 | tf_op jit(solution)/shard_map/reduce_scatter | solution.py:51
  148.8 0.9 fusion.83
  149.7 1.1 stack.9
  150.8 9.4 %all-to-all-start.1 = ((f32[16,32,512]{2,1,0:T(8,128)}), f32[16,32,512]{2,1,0:T(8,128)S(1)}, u32[]{:S(2)}, u32[]{:S(2)}) async-start(f32[16,32,512]{2,1,0:T(8,128)} %stack.9), calls=%async_computation.2 | async-start | bytes 2097152 | tf_op jit(solution)/shard_map/all_to_all | solution.py:47
  160.2 27.9 %all-to-all-done.1 = f32[16,32,512]{2,1,0:T(8,128)S(1)} async-done(((f32[16,32,512]{2,1,0:T(8,128)}), f32[16,32,512]{2,1,0:T(8,128)S(1)}, u32[]{:S(2)}, u32[]{:S(2)}) %all-to-all-start.1) | async-done | bytes 1048608 | tf_op jit(solution)/shard_map/all_to_all | solution.py:47
  189.7 23.8 %while.45 = (s32[]{:T(128)}, f32[32,32,256]{2,1,0:T(8,128)S(1)}, s32[]{:T(128)}, f32[32,256,256]{2,1,0:T(8,128)}, s32[32]{0:T(128)S(1)}, /*index=5*/f32[32,32,25...) while((s32[]{:T(128)}, f32[32,32,256]{2,1,0:T(8,128)S(1)}, ...), condition=%wide.region_4.6_spmd.clone, body=%wide.region_3.5_spmd.clone.sunk | while | flops 226821696 | bytes 5509559 | solution.py:29
  191.0 3.6 fusion.128
  194.7 0.9 fusion.129
  197.0 3.6 fusion.128
  200.7 0.9 fusion.129
  202.9 3.6 fusion.128
  206.6 0.9 fusion.129
  208.8 3.6 fusion.128
  212.6 0.9 fusion.129
  213.5 1.6 copy.51
  215.1 72.7 %reduce-scatter.7.cloned.1.call-done = f32[32,512]{1,0:T(8,128)} async-done(((f32[32,8192]{1,0:T(8,128)}), f32[32,512]{1,0:T(8,128)}) %reduce-scatter.7.cloned.1.call-update) | async-done | bytes 65552 | tf_op jit(solution)/shard_map/reduce_scatter | solution.py:51
  287.8 0.9 multiply_subtract_fusion.1
  288.7 1.1 stack.10
  289.8 9.3 %all-to-all-start.2 = ((f32[16,32,512]{2,1,0:T(8,128)}), f32[16,32,512]{2,1,0:T(8,128)S(1)}, u32[]{:S(2)}, u32[]{:S(2)}) async-start(f32[16,32,512]{2,1,0:T(8,128)} %stack.10), calls=%async_computation.4 | async-start | bytes 2097152 | tf_op jit(solution)/shard_map/all_to_all | solution.py:47
  299.3 27.8 %all-to-all-done.2 = f32[16,32,512]{2,1,0:T(8,128)S(1)} async-done(((f32[16,32,512]{2,1,0:T(8,128)}), f32[16,32,512]{2,1,0:T(8,128)S(1)}, u32[]{:S(2)}, u32[]{:S(2)}) %all-to-all-start.2) | async-done | bytes 1048608 | tf_op jit(solution)/shard_map/all_to_all | solution.py:47
  328.6 23.8 %while.46 = (s32[]{:T(128)}, f32[32,32,256]{2,1,0:T(8,128)S(1)}, s32[]{:T(128)}, f32[32,256,256]{2,1,0:T(8,128)}, s32[32]{0:T(128)S(1)}, /*index=5*/f32[32,32,25...) while((s32[]{:T(128)}, f32[32,32,256]{2,1,0:T(8,128)S(1)}, ...), condition=%wide.region_7.9_spmd.clone, body=%wide.region_6.8_spmd.clone.sunk | while | flops 226821696 | bytes 5509559 | solution.py:29
  330.0 3.6 fusion.134
  333.7 0.9 fusion.135
  335.9 3.6 fusion.134
  339.6 0.9 fusion.135
  341.8 3.6 fusion.134
  345.6 0.9 fusion.135
  347.8 3.6 fusion.134
  351.5 0.9 fusion.135
  352.4 1.6 copy.52
  354.0 72.7 %reduce-scatter.9.cloned.1.call-done = f32[32,512]{1,0:T(8,128)} async-done(((f32[32,8192]{1,0:T(8,128)}), f32[32,512]{1,0:T(8,128)}) %reduce-scatter.9.cloned.1.call-update) | async-done | bytes 65552 | tf_op jit(solution)/shard_map/reduce_scatter | solution.py:51
  426.7 0.9 multiply_subtract_fusion
  427.8 77.3 %psum.14 = f32[32,32]{0,1:T(8,128)S(1)} all-reduce(f32[32,32]{0,1:T(8,128)S(1)} %fusion.89), channel_id=1, replica_groups=mesh['row'=16,'col'=16] {'row','col'}, use_global_device_ids=true, to_apply=%region_9.11 | all-reduce | flops 1024 | bytes 8192 | tf_op jit(solution)/shard_map/psum | solution.py:64
  505.2 2.9 cholesky.16
  509.5 2.4 custom-call.7
  512.2 1.1 stack.11
  513.3 6.6 all-to-all-start.3
  520.0 27.9 %all-to-all-done.3 = f32[16,32,512]{2,1,0:T(8,128)S(1)} async-done(((f32[16,32,512]{2,1,0:T(8,128)}), f32[16,32,512]{2,1,0:T(8,128)S(1)}, u32[]{:S(2)}, u32[]{:S(2)}) %all-to-all-start.3) | async-done | bytes 1048608 | tf_op jit(solution)/shard_map/all_to_all | solution.py:47
  549.4 23.8 %while.47 = (s32[]{:T(128)}, f32[32,32,256]{2,1,0:T(8,128)S(1)}, s32[]{:T(128)}, f32[32,256,256]{2,1,0:T(8,128)}, s32[32]{0:T(128)S(1)}, /*index=5*/f32[32,32,25...) while((s32[]{:T(128)}, f32[32,32,256]{2,1,0:T(8,128)S(1)}, ...), condition=%wide.region_13.15_spmd.clone, body=%wide.region_12.14_spmd.clone.sunk | while | flops 226821696 | bytes 5509559 | solution.py:29
  550.8 3.6 fusion.140
  554.5 0.9 fusion.141
  556.7 3.6 fusion.140
  560.4 0.9 fusion.141
  562.6 3.6 fusion.140
  566.4 0.9 fusion.141
  568.6 3.6 fusion.140
  572.3 0.9 fusion.141
  573.2 1.6 copy.53
  574.8 70.8 %reduce-scatter.11.cloned.1.call-done = f32[32,512]{1,0:T(8,128)} async-done(((f32[32,8192]{1,0:T(8,128)}), f32[32,512]{1,0:T(8,128)}) %reduce-scatter.11.cloned.1.call-update) | async-done | bytes 65552 | tf_op jit(solution)/shard_map/reduce_scatter | solution.py:51
  645.7 1.0 fusion.80
  646.7 77.3 %psum.15 = f32[32,32]{0,1:T(8,128)S(1)} all-reduce(f32[32,32]{0,1:T(8,128)S(1)} %fusion.80), channel_id=1, replica_groups=mesh['row'=16,'col'=16] {'row','col'}, use_global_device_ids=true, to_apply=%region_15.17 | all-reduce | flops 1024 | bytes 8192 | tf_op jit(solution)/shard_map/psum | solution.py:68
  (114 shorter events, 31.1 us)
Async XLA Ops:
  7.2 41.5 %copy-start.3 = (s32[1,32]{1,0:T(1,128)S(1)}, s32[1,32]{1,0:T(1,128)}, u32[]{:S(2)}) copy-start(s32[1,32]{1,0:T(1,128)} %param.20) | copy-start | bytes 388
  7.2 41.5 %copy-start.5 = (s32[1,32]{1,0:T(1,128)S(1)}, s32[1,32]{1,0:T(1,128)}, u32[]{:S(2)}) copy-start(s32[1,32]{1,0:T(1,128)} %param.19) | copy-start | bytes 388
  9.1 38.0 %all-to-all-start = ((f32[16,32,512]{2,1,0:T(8,128)}), f32[16,32,512]{2,1,0:T(8,128)S(1)}, u32[]{:S(2)}, u32[]{:S(2)}) async-start(f32[16,32,512]{2,1,0:T(8,128)} %stack.8), calls=%async_computation | async-start | bytes 2097152 | tf_op jit(solution)/shard_map/all_to_all | solution.py:47
  19.1 129.7 %reduce-scatter.5.cloned.1.call-start = ((), (), s32[]{:S(2)}) async-start(), calls=%async_computation.8 | async-start | bytes 1114112 | tf_op jit(solution)/shard_map/reduce_scatter | solution.py:51
  48.6 100.2 %copy-start = (f32[32,512]{1,0:T(8,128)S(1)}, f32[32,512]{1,0:T(8,128)}, u32[]{:S(2)}) copy-start(f32[32,512]{1,0:T(8,128)} %param.16) | copy-start | bytes 196612
  48.6 100.2 %copy-start.4 = (f32[512]{0:T(512)S(1)}, f32[512]{0:T(512)}, u32[]{:S(2)}) copy-start(f32[512]{0:T(512)} %param.17) | copy-start | bytes 6148
  150.8 37.4 %all-to-all-start.1 = ((f32[16,32,512]{2,1,0:T(8,128)}), f32[16,32,512]{2,1,0:T(8,128)S(1)}, u32[]{:S(2)}, u32[]{:S(2)}) async-start(f32[16,32,512]{2,1,0:T(8,128)} %stack.9), calls=%async_computation.2 | async-start | bytes 2097152 | tf_op jit(solution)/shard_map/all_to_all | solution.py:47
  160.2 127.6 %reduce-scatter.7.cloned.1.call-start = ((), (), s32[]{:S(2)}) async-start(), calls=%async_computation.9 | async-start | bytes 1114112 | tf_op jit(solution)/shard_map/reduce_scatter | solution.py:51
  189.7 98.1 %copy-start.2 = (f32[32,512]{1,0:T(8,128)S(1)}, f32[32,512]{1,0:T(8,128)}, u32[]{:S(2)}) copy-start(f32[32,512]{1,0:T(8,128)} %reduce-scatter.5.cloned.1.call-done) | copy-start | bytes 196612
  289.8 37.3 %all-to-all-start.2 = ((f32[16,32,512]{2,1,0:T(8,128)}), f32[16,32,512]{2,1,0:T(8,128)S(1)}, u32[]{:S(2)}, u32[]{:S(2)}) async-start(f32[16,32,512]{2,1,0:T(8,128)} %stack.10), calls=%async_computation.4 | async-start | bytes 2097152 | tf_op jit(solution)/shard_map/all_to_all | solution.py:47
  299.1 127.6 %reduce-scatter.9.cloned.1.call-start = ((), (), s32[]{:S(2)}) async-start(), calls=%async_computation.10 | async-start | bytes 1114112 | tf_op jit(solution)/shard_map/reduce_scatter | solution.py:51
  512.2 133.5 %copy-start.1 = (f32[32,512]{1,0:T(8,128)}, f32[32,512]{1,0:T(8,128)S(1)}, u32[]{:S(2)}) copy-start(f32[32,512]{1,0:T(8,128)S(1)} %fusion.87) | copy-start | bytes 196612
  513.3 34.6 %all-to-all-start.3 = ((f32[16,32,512]{2,1,0:T(8,128)}), f32[16,32,512]{2,1,0:T(8,128)S(1)}, u32[]{:S(2)}, u32[]{:S(2)}) async-start(f32[16,32,512]{2,1,0:T(8,128)} %stack.11), calls=%async_computation.6 | async-start | bytes 2097152 | tf_op jit(solution)/shard_map/all_to_all | solution.py:47
  519.9 125.7 %reduce-scatter.11.cloned.1.call-start = ((), (), s32[]{:S(2)}) async-start(), calls=%async_computation.11 | async-start | bytes 1114112 | tf_op jit(solution)/shard_map/reduce_scatter | solution.py:51
Sparse Core Ops, SparseCore 0:
  74.2 74.5 reduce-scatter.4
  215.2 72.5 reduce-scatter.6
  354.1 72.4 reduce-scatter.8
  574.9 70.6 reduce-scatter.10
